TPU v7x, 512 devices: a whole 4x8x8 slice. The times are simulated.
512 devices in a mesh: ep: 128 (over y, z, core), rep: 4 (over x).
Axes of the slice: x: 4, y: 8, z: 8, core: 2. Of those that a mesh axis runs over, the one named last changes fastest.
Arguments:
- tokens: bfloat16 [2048, 3584], P('ep', 'rep'), may hold values from -6 to 6
- expert_ids: int32 [2048, 8], P('ep'), may hold values from 0 to 127, all different within a row; in each aligned block of 16 rows (0 to 15, 16 to 31, ...) at most 2 rows name the same one
- gate_weights: float32 [2048, 8], P('ep'), may hold values from 0.05 to 0.5
- up_weight: bfloat16 [128, 3584, 1024], P('ep', 'rep'), may hold values from -0.09375 to 0.09375
- down_weight: bfloat16 [128, 1024, 3584], P('ep', None, 'rep'), may hold values from -0.1875 to 0.1875
Outputs:
- mixture: bfloat16 [2048, 3584], P('ep', 'rep')
Inputs may be any that keep to these rules, and one draw needn't show every extreme that they name: `expert_ids`: the 8 experts of a token differ. Within the rows of one device (each aligned block of 16 tokens) no expert is named by more than 2 tokens, a bound that some block reaches.
All inputs are finite; a program needn't handle non-finite values.
Results may differ from a plain program's by a relative error of at most 0.017.
Values may be sent and summed in bfloat16 or wider, within the bound.
A program may use at most 64 MiB of HBM per device.

v0:
```python
import jax
import jax.numpy as jnp
from jax import lax
from jax.sharding import PartitionSpec as P


def local(tokens, expert_ids, gate_weights, up_weight, down_weight):
    n_peers = lax.axis_size("ep")
    tok_rows, top_count = expert_ids.shape
    width_part = tokens.shape[1]
    capacity = min(tok_rows, max(2, 3 * tok_rows * top_count // (2 * n_peers)))
    flat_ids = expert_ids.reshape(-1)
    onehot = (flat_ids[:, None] == jnp.arange(n_peers, dtype=jnp.int32)[None, :]).astype(jnp.int32)
    before = jnp.cumsum(onehot, axis=0) - onehot
    ranking = jnp.sum(before * onehot, axis=1)
    slot_index = flat_ids * capacity + ranking
    token_of_row = jnp.arange(tok_rows * top_count, dtype=jnp.int32) // top_count
    outbound = (
        jnp.zeros((n_peers * capacity, width_part), tokens.dtype)
        .at[slot_index]
        .set(tokens[token_of_row])
    )
    inbound = lax.all_to_all(outbound, "ep", split_axis=0, concat_axis=0, tiled=True)
    up_local = up_weight[0]
    down_local = down_weight[0]
    partial_pre = jnp.dot(inbound, up_local, preferred_element_type=jnp.float32)
    pre_total = lax.psum(partial_pre.astype(jnp.bfloat16), "rep").astype(jnp.float32)
    hidden = jax.nn.silu(pre_total).astype(jnp.bfloat16)
    expert_out = jnp.dot(hidden, down_local, preferred_element_type=jnp.float32).astype(
        jnp.bfloat16
    )
    returned = lax.all_to_all(expert_out, "ep", split_axis=0, concat_axis=0, tiled=True)
    picked = returned[slot_index].astype(jnp.float32).reshape(tok_rows, top_count, width_part)
    mixture = jnp.sum(gate_weights[:, :, None] * picked, axis=1)
    return mixture.astype(jnp.bfloat16)


def solution(mesh):
    placed = (
        P("ep", "rep"),
        P("ep", None),
        P("ep", None),
        P("ep", "rep", None),
        P("ep", None, "rep"),
    )
    return jax.shard_map(
        local, mesh=mesh, in_specs=placed, out_specs=P("ep", "rep"), check_vma=False
    )
```

profile of v0, /device:TPU:1, one launch (start us, length us, event | category | flops | bytes accessed | tf_op | source)
XLA Modules:
  0.0 142.5 jit_solution(13055652494298791884)
XLA Ops:
  6.5 0.0 copy-start
  6.5 0.0 all-reduce.2.cloned.1.call-start
  6.5 0.9 copy.11
  7.4 0.7 broadcast_multiply_fusion
  8.1 0.1 eq.15
  8.2 0.1 fusion.20
  8.3 0.2 reduce_window_sum.11
  8.5 0.2 select_reduce_fusion
  8.7 0.1 copy.10
  8.7 0.1 mul.34
  8.9 3.2 %scatter_custom_fusion = bf16[256,896]{1,0:T(8,128)(2,1)S(1)} fusion(s32[128]{0:T(128)S(1)} %fusion.22, bf16[16,896]{1,0:T(8,128)(2,1)} %param.5, s32[1024]{0:T(1024)S(1)} %pad_clamp_fusion.1, bf16[]{:T(256)} %constant.26.clone.1), kind=kCustom, calls=%fused_computation.18 | custom fusion | bytes 459264 | tf_op jit(solution)/shard_map/scatter | solution.py:21
  12.1 0.2 all_to_all.16
  12.3 36.4 %all_to_all.24 = bf16[128,2,896]{2,1,0:T(2,128)(2,1)S(1)} all-to-all(bf16[128,2,896]{2,1,0:T(2,128)(2,1)S(1)} %all_to_all.16), channel_id=1, replica_groups=mesh['ep'=128,'rep'=4] {'ep'}, dimensions={0} | all-to-all | bytes 917504 | tf_op jit(solution)/shard_map/all_to_all | solution.py:23
  48.7 0.2 all_to_all.18
  48.9 0.0 copy-done
  48.9 1.6 %fusion.4 = bf16[256,1024]{1,0:T(8,128)(2,1)} fusion(bf16[256,896]{1,0:T(8,128)(2,1)S(1)} %all_to_all.18, bf16[1,896,1024]{2,1,0:T(8,128)(2,1)S(1)} %copy-done), kind=kOutput, calls=%fused_computation.9 | convolution fusion | flops 470024192 | bytes 2818048 | tf_op jit(solution)/shard_map/dot_general | solution.py:26
  50.5 0.0 all-reduce.2.cloned.1.call-update
  50.5 45.2 %all-reduce.2.cloned.1.call-done = bf16[256,1024]{1,0:T(8,128)(2,1)} async-done(((bf16[256,1024]{1,0:T(8,128)(2,1)}), bf16[256,1024]{1,0:T(8,128)(2,1)}) %all-reduce.2.cloned.1.call-update) | async-done | bytes 524304 | tf_op jit(solution)/shard_map/psum | solution.py:27
  95.7 2.4 %fusion.7 = bf16[256,896]{1,0:T(8,128)(2,1)S(1)} fusion(bf16[1,1024,896]{2,1,0:T(8,128)(2,1)} %param.9, bf16[256,1024]{1,0:T(8,128)(2,1)} %all-reduce.2.cloned.1.call-done), kind=kOutput, calls=%fused_computation.10 | convolution fusion | flops 471564288 | bytes 2818048 | tf_op jit(solution)/shard_map/dot_general | solution.py:29
  98.1 0.0 copy-start.1
  98.1 0.9 all_to_all.19
  99.0 16.5 %all-to-all-start.1 = ((bf16[128,2,896]{2,1,0:T(2,128)(2,1)}), bf16[128,2,896]{2,1,0:T(2,128)(2,1)S(1)}, u32[]{:S(2)}, u32[]{:S(2)}) async-start(bf16[128,2,896]{2,1,0:T(2,128)(2,1)} %all_to_all.19), calls=%async_computation.1 | async-start | bytes 917504 | tf_op jit(solution)/shard_map/all_to_all | solution.py:32
  115.5 0.0 copy-done.1
  115.5 0.1 copy.9
  115.6 18.1 %all-to-all-done.1 = bf16[128,2,896]{2,1,0:T(2,128)(2,1)S(1)} async-done(((bf16[128,2,896]{2,1,0:T(2,128)(2,1)}), bf16[128,2,896]{2,1,0:T(2,128)(2,1)S(1)}, u32[]{:S(2)}, u32[]{:S(2)}) %all-to-all-start.1) | async-done | bytes 458784 | tf_op jit(solution)/shard_map/all_to_all | solution.py:32
  133.7 0.2 all_to_all.21
  133.9 0.9 gather_fusion
  134.8 0.8 fusion.16
  (4 shorter events, 0.0 us)
Async XLA Ops:
  6.5 42.3 %copy-start = (bf16[1,896,1024]{2,1,0:T(8,128)(2,1)S(1)}, bf16[1,896,1024]{2,1,0:T(8,128)(2,1)}, u32[]{:S(2)}) copy-start(bf16[1,896,1024]{2,1,0:T(8,128)(2,1)} %param.8) | copy-start | bytes 5505028
  6.5 89.1 %all-reduce.2.cloned.1.call-start = ((), (), s32[]{:S(2)}) async-start(), calls=%async_computation.2 | async-start | bytes 1048576 | tf_op jit(solution)/shard_map/psum | solution.py:27
  98.1 17.4 %copy-start.1 = (f32[16,8]{0,1:T(8,128)S(1)}, f32[16,8]{0,1:T(8,128)}, u32[]{:S(2)}) copy-start(f32[16,8]{0,1:T(8,128)} %param.7) | copy-start | bytes 1540
  99.0 34.7 %all-to-all-start.1 = ((bf16[128,2,896]{2,1,0:T(2,128)(2,1)}), bf16[128,2,896]{2,1,0:T(2,128)(2,1)S(1)}, u32[]{:S(2)}, u32[]{:S(2)}) async-start(bf16[128,2,896]{2,1,0:T(2,128)(2,1)} %all_to_all.19), calls=%async_computation.1 | async-start | bytes 917504 | tf_op jit(solution)/shard_map/all_to_all | solution.py:32
Sparse Core Ops, SparseCore 0:
  50.6 45.0 all-reduce.1
where the time goes:
time: 143 us; the launch traced here: 142 us
  waiting for transfers between devices  63.3 us (44%)
  blocking collectives  36.4 us (25%)
  starting transfers between devices  16.5 us (12%)
  between operations  13.5 us (9%)
  local copies, waits for them, and re-layouts  6.8 us (5%)
  matrix products  3.98 us (3%)
  other arithmetic  1.97 us (1%)
    psum x1, waiting for transfers between devices, local(): lax.psum(partial_pre.astype(jnp.bfloat16), 'rep').astype(jnp.float32)  45.2 us
    all_to_all x1, blocking collectives, local(): lax.all_to_all(outbound, 'ep', split_axis=0, concat_axis=0, tiled=True)  36.4 us
    all_to_all x1, waiting for transfers between devices, local(): lax.all_to_all(expert_out, 'ep', split_axis=0, concat_axis=0, tiled=True)  18.1 us
    all_to_all x1, starting transfers between devices, local(): lax.all_to_all(expert_out, 'ep', split_axis=0, concat_axis=0, tiled=True)  16.5 us
    scatter x1, local copies, waits for them, and re-layouts, local(): outbound = jnp.zeros((n_peers * capacity, width_part), tokens.dtype).at[s...  3.23 us
  transfers between devices with their start and end apart: 2, of which 2 were waited for; matrix products, arithmetic and copies ran while one was open for 0% of the time, Pallas kernels for 0%

commit v1 on v0

v1 whole, which is shorter than its diff:
```python
import functools

import jax
import jax.numpy as jnp
from jax import lax
from jax.experimental import pallas as pl
from jax.experimental.pallas import tpu as pltpu
from jax.sharding import PartitionSpec as P

MESH = pl.DeviceIdType.MESH
F32, BF16 = jnp.float32, jnp.bfloat16


def far_first(n):
    return sorted(range(1, n), key=lambda s: -min(s, n - s))


def dot(a, b, ca, cb):
    return lax.dot_general(a, b, (((ca,), (cb,)), ((), ())), preferred_element_type=F32)


def iota(shape, dim):
    return lax.broadcasted_iota(jnp.int32, shape, dim)


def kernel(
    side, reps, ids_hbm, gates_hbm, tok_hbm, up_hbm, down_hbm, out_ref,
    ids_v, gates_v, up_v, down_v, told, picked, inbound, part, gathered, hid, acc,
    sent, back, mixed, shares,
    s_load, s_bc, r_bc, s_pick, r_pick, s_part, r_part, s_hid, r_hid, s_out, r_out, s_mix, r_mix,
):
    top, toks = ids_v.shape
    experts = 2 * side * side
    width = tok_hbm.shape[1]
    chunks = s_part.shape[1]
    ffc = up_v.shape[1] // chunks
    lines = 2 * side
    rows = lines * lines
    e = lax.axis_index("ep")
    x = lax.axis_index("rep")
    y, z, c = e // (2 * side), (e // 2) % side, e % 2
    p, q = y * (1 - c) + z * c, z * (1 - c) + y * c
    sp = 2 * side * (1 - c) + 2 * c
    sq = 2 * (1 - c) + 2 * side * c

    def mod(v, n):
        return lax.rem(v, n)

    barrier = pltpu.get_barrier_semaphore()

    def greet(ep, rep):
        pl.semaphore_signal(barrier, inc=1, device_id=(ep, rep), device_id_type=MESH)

    for s in far_first(side):
        for core in range(2):
            greet(y * 2 * side + mod(z + s, side) * 2 + core, x)
            greet(mod(y + s, side) * 2 * side + z * 2 + core, x)
    greet(e + 1 - 2 * c, x)
    for s in far_first(reps):
        greet(e, mod(x + s, reps))

    loads = [
        pltpu.make_async_copy(ids_hbm, ids_v, s_load.at[0]),
        pltpu.make_async_copy(gates_hbm, gates_v, s_load.at[1]),
        pltpu.make_async_copy(tok_hbm, told.at[p, :, pl.ds(0, width)], s_load.at[2]),
        pltpu.make_async_copy(up_hbm.at[0], up_v, s_load.at[3]),
        pltpu.make_async_copy(down_hbm.at[0], down_v, s_load.at[4]),
    ]
    for load in loads:
        load.start()

    loads[0].wait()
    loads[1].wait()
    ids, gates = ids_v[...], gates_v[...]
    which = iota((experts, toks), 0)
    named = jnp.zeros((experts, toks), F32)
    gate = jnp.zeros((experts, toks), F32)
    for k in range(top):
        same = which == ids[k:k + 1, :]
        named = jnp.where(same, 1.0, named)
        gate = jnp.where(same, gates[k:k + 1, :], gate)
    earlier = (iota((toks, toks), 0) < iota((toks, toks), 1)).astype(BF16)
    rank = dot(named.astype(BF16), earlier, 1, 0)
    code = jnp.where(rank > 0.5, -gate, gate).astype(BF16)
    eye = (iota((experts, experts), 0) == iota((experts, experts), 1)).astype(BF16)
    told[p, :, width:] = dot(code, eye, 0, 0).astype(BF16)
    loads[2].wait()

    pl.semaphore_wait(barrier, 4 * (side - 1) + 1 + reps - 1)

    spread = []
    for s in far_first(side):
        to = mod(p + s, side)
        spread.append(pltpu.make_async_remote_copy(
            src_ref=told.at[p], dst_ref=told.at[p], send_sem=s_bc.at[s], recv_sem=r_bc.at[p],
            device_id=(to * sp + q * sq + c, x), device_id_type=MESH))
        spread[-1].start()

    def arrival(ref, sem):
        pltpu.make_async_copy(ref, ref, sem).wait()

    for s in far_first(side):
        frm = mod(p + s, side)
        arrival(told.at[frm], r_bc.at[frm])

    held = told[...].reshape(side * toks, width + experts)
    codes = held[:, width:]

    def expert_of(col):
        block = col // lines
        return p * sp + (block // 2) * sq + block % 2

    col, tok = iota((rows, side * toks), 0), iota((rows, side * toks), 1)
    sel = (expert_of(iota((rows, experts), 0)) == iota((rows, experts), 1)).astype(BF16)
    value = dot(sel, codes, 1, 1)
    sign = (1 - 2 * (col % 2)).astype(F32)
    hit = (value * sign > 0.0) & ((col % lines) // 2 == tok // toks)
    pick = jnp.where(hit, 1.0, 0.0).astype(BF16)
    picked[...] = dot(pick, held[:, :width], 1, 0).astype(BF16).reshape(lines, lines, width)

    group = c * side + q
    own = q * 2 + c
    send_pick = []
    for s in far_first(side) + [0]:
        for core in range(2):
            if s == 0 and core == 1:
                continue
            to = mod(q + s, side)
            core_to = mod(c + core, 2) if s else 1 - c
            send_pick.append(pltpu.make_async_remote_copy(
                src_ref=picked.at[to * 2 + core_to], dst_ref=inbound.at[group],
                send_sem=s_pick.at[s * 2 + core], recv_sem=r_pick.at[group],
                device_id=(p * sp + to * sq + core_to, x), device_id_type=MESH))
            send_pick[-1].start()
    inbound[group] = picked[own]

    col, tok = iota((side * toks, rows), 1), iota((side * toks, rows), 0)
    sel = (expert_of(iota((experts, rows), 1)) == iota((experts, rows), 0)).astype(BF16)
    value = dot(codes, sel, 1, 0) * (1 - 2 * (col % 2)).astype(F32)
    hit = (value > 0.0) & ((col % lines) // 2 == tok // toks)
    weight = jnp.where(hit, value, 0.0).astype(BF16)

    for s in range(1, lines):
        frm = mod(group + s, lines)
        arrival(inbound.at[frm], r_pick.at[frm])

    per = rows // reps
    loads[3].wait()
    lhs = inbound[...].reshape(rows, width)
    send_part = []
    for n in range(chunks):
        cols = pl.ds(n * ffc, ffc)
        block = dot(lhs, up_v[:, cols], 1, 0).astype(BF16).reshape(reps, per, ffc)
        part[:, :, cols] = block
        for s in far_first(reps):
            to = mod(x + s, reps)
            send_part.append(pltpu.make_async_remote_copy(
                src_ref=part.at[to, :, cols], dst_ref=gathered.at[x, :, cols],
                send_sem=s_part.at[s, n], recv_sem=r_part.at[x, n],
                device_id=(e, to), device_id_type=MESH))
            send_part[-1].start()
        gathered[x, :, cols] = part[x, :, cols]

    send_hid = []
    for n in range(chunks):
        cols = pl.ds(n * ffc, ffc)
        for s in range(1, reps):
            frm = mod(x + s, reps)
            arrival(gathered.at[frm, :, cols], r_part.at[frm, n])
        pre = gathered[0, :, cols].astype(F32)
        for r in range(1, reps):
            pre = pre + gathered[r, :, cols].astype(F32)
        hid[x, :, cols] = (pre / (1.0 + jnp.exp(-pre))).astype(BF16)
        for s in far_first(reps):
            send_hid.append(pltpu.make_async_remote_copy(
                src_ref=hid.at[x, :, cols], dst_ref=hid.at[x, :, cols],
                send_sem=s_hid.at[s, n], recv_sem=r_hid.at[x, n],
                device_id=(e, mod(x + s, reps)), device_id_type=MESH))
            send_hid[-1].start()

    loads[4].wait()
    for n in range(chunks):
        cols = pl.ds(n * ffc, ffc)
        for s in range(1, reps):
            frm = mod(x + s, reps)
            arrival(hid.at[frm, :, cols], r_hid.at[frm, n])
        term = dot(hid[:, :, cols].reshape(rows, ffc), down_v[cols, :], 1, 0)
        if n == 0:
            acc[...] = term
        elif n < chunks - 1:
            acc[...] += term
        else:
            sent[...] = (acc[...] + term).astype(BF16).reshape(lines, lines, width)

    send_out = []

    def to_relay(slot, block, place, device):
        send_out.append(pltpu.make_async_remote_copy(
            src_ref=sent.at[block], dst_ref=back.at[place], send_sem=s_out.at[slot], recv_sem=r_out.at[place],
            device_id=(device, x), device_id_type=MESH))
        send_out[-1].start()

    for s in far_first(side) + [0]:
        if s:
            to = mod(q + s, side)
            to_relay(2 * s, c * side + to, own, p * sp + to * sq + c)
        to = mod(p + s, side)
        to_relay(2 * s + 1, (1 - c) * side + to, p * 2 + c, to * sp + q * sq + 1 - c)
    back[own] = sent[group]
    for s in range(1, lines):
        frm = mod(own + s, lines)
        arrival(back.at[frm], r_out.at[frm])

    mixed[...] = dot(weight, back[...].reshape(rows, width), 1, 0).astype(BF16).reshape(side, toks, width)
    send_mix = []
    for s in far_first(side):
        to = mod(p + s, side)
        send_mix.append(pltpu.make_async_remote_copy(
            src_ref=mixed.at[to], dst_ref=shares.at[p], send_sem=s_mix.at[s], recv_sem=r_mix.at[p],
            device_id=(to * sp + q * sq + c, x), device_id_type=MESH))
        send_mix[-1].start()
    shares[p] = mixed[p]
    for s in range(1, side):
        frm = mod(p + s, side)
        arrival(shares.at[frm], r_mix.at[frm])
    total = shares[0].astype(F32)
    for k in range(1, side):
        total = total + shares[k].astype(F32)
    out_ref[...] = total.astype(BF16)

    for copy in spread + send_pick + send_part + send_hid + send_out + send_mix:
        copy.wait_send()


def local(side, reps, chunks, tokens, expert_ids, gate_weights, up_weight, down_weight):
    toks, top = expert_ids.shape
    width = tokens.shape[1]
    ff = up_weight.shape[2]
    experts = 2 * side * side
    lines = 2 * side
    rows = lines * lines
    anywhere = pl.BlockSpec(memory_space=pl.ANY)
    dma = pltpu.SemaphoreType.DMA
    vmem = pltpu.VMEM
    return pl.pallas_call(
        functools.partial(kernel, side, reps),
        out_shape=jax.ShapeDtypeStruct((toks, width), BF16),
        in_specs=[anywhere] * 5,
        out_specs=pl.BlockSpec(memory_space=pltpu.VMEM),
        scratch_shapes=[
            vmem((top, toks), jnp.int32),
            vmem((top, toks), F32),
            vmem((width, ff), BF16),
            vmem((ff, width), BF16),
            vmem((side, toks, width + experts), BF16),
            vmem((lines, lines, width), BF16),
            vmem((lines, lines, width), BF16),
            vmem((reps, rows // reps, ff), BF16),
            vmem((reps, rows // reps, ff), BF16),
            vmem((reps, rows // reps, ff), BF16),
            vmem((rows, width), F32),
            vmem((lines, lines, width), BF16),
            vmem((lines, lines, width), BF16),
            vmem((side, toks, width), BF16),
            vmem((side, toks, width), BF16),
            dma((5,)),
            dma((side,)), dma((side,)),
            dma((lines,)), dma((lines,)),
            dma((reps, chunks)), dma((reps, chunks)),
            dma((reps, chunks)), dma((reps, chunks)),
            dma((lines,)), dma((lines,)),
            dma((side,)), dma((side,)),
        ],
        compiler_params=pltpu.CompilerParams(
            collective_id=0, has_side_effects=True, vmem_limit_bytes=56 * 1024 * 1024),
    )(expert_ids.T, gate_weights.T, tokens, up_weight, down_weight)


def solution(mesh):
    side = round((mesh.shape["ep"] // 2) ** 0.5)
    placed = (
        P("ep", "rep"),
        P("ep", None),
        P("ep", None),
        P("ep", "rep", None),
        P("ep", None, "rep"),
    )
    return jax.shard_map(
        functools.partial(local, side, mesh.shape["rep"], 4),
        mesh=mesh, in_specs=placed, out_specs=P("ep", "rep"), check_vma=False
    )
```

time: 143 us -> 59.7 us (0.42)
  waiting for transfers between devices: 63.3 us -> 0 us
  Pallas kernels: 0 us -> 58.1 us
  blocking collectives: 36.4 us -> 0 us
  starting transfers between devices: 16.5 us -> 0 us
  between operations: 13.5 us -> 0.01 us
  local copies, waits for them, and re-layouts: 6.8 us -> 1.36 us
  matrix products: 3.98 us -> 0 us
  other arithmetic: 1.97 us -> 0 us
    pallas_call x0 -> x1, Pallas kernels: none -> 58.1 us  [local(): pl.pallas_call(functools.partial(kernel, side, reps), out_shape=jax.Shape...]
    psum x1 -> x0, waiting for transfers between devices: 45.2 us -> none  [local(): lax.psum(partial_pre.astype(jnp.bfloat16), 'rep').astype(jnp.float32)]
    all_to_all x1 -> x0, blocking collectives: 36.4 us -> none  [local(): lax.all_to_all(outbound, 'ep', split_axis=0, concat_axis=0, tiled=True)]
    all_to_all x1 -> x0, waiting for transfers between devices: 18.1 us -> none  [local(): lax.all_to_all(expert_out, 'ep', split_axis=0, concat_axis=0, tiled=True)]
    all_to_all x1 -> x0, starting transfers between devices: 16.5 us -> none  [local(): lax.all_to_all(expert_out, 'ep', split_axis=0, concat_axis=0, tiled=True)]
    dot_general x2 -> x0, matrix products: 3.98 us -> none  [the longest x1 2.42 us: local(): jnp.dot(hidden, down_local, preferred_element_type=jnp.float32)]
    scatter x1 -> x0, local copies, waits for them, and re-layouts: 3.23 us -> none  [local(): outbound = jnp.zeros((n_peers * capacity, width_part), tokens.dtype).at[s...]
    all_to_all x4 -> x0, local copies, waits for them, and re-layouts: 1.46 us -> none  [the longest x2 1.12 us: local(): lax.all_to_all(expert_out, 'ep', split_axis=0, concat_axis=0, tiled=True)]
  transfers between devices with their start and end apart: 2 -> 0, of which waited for: 2 -> 0; matrix products, arithmetic and copies ran while one was open for 0% -> 0% of each run, Pallas kernels for 0% -> 0%
where the time goes in v1:
time: 59.7 us; the launch traced here: 59.5 us
  Pallas kernels  58.1 us (97%)
  local copies, waits for them, and re-layouts  1.36 us (2%)
    pallas_call x1, Pallas kernels, local(): pl.pallas_call(functools.partial(kernel, side, reps), out_shape=jax.Shape...  58.1 us
    unnamed x1, local copies, waits for them, and re-layouts  1.36 us

profile of v1, /device:TPU:1, one launch (start us, length us, event | category | flops | bytes accessed | tf_op | source)
XLA Modules:
  0.0 59.5 jit_solution(13459003243693947357)
XLA Ops:
  0.0 58.1 %shard_map.55 = bf16[16,896]{1,0:T(8,128)(2,1)} custom-call(s32[8,16]{1,0:T(8,128)} %bitcast.2, f32[8,16]{1,0:T(8,128)} %bitcast.3, bf16[16,896]{1,0:T(8,128)(2,1)} %tok_hbm.1, bf16[1,896,1024]{2,1,0:T(8,128)(2,1)} %up_hbm.1, bf16[1,1024,896]{2,1,0:T(8,128)(2,1)} %down_hbm.1), custom_call_target="tpu_custom_call" | custom-call | tf_op jit(solution)/shard_map/pallas_call | solution.py:245
  58.1 1.4 %copy.7 = bf16[16,896]{1,0:T(8,128)(2,1)} copy(bf16[16,896]{1,0:T(8,128)(2,1)} %shard_map.55) | data formatting | bytes 57344

commit v2 on v0

v2 whole, which is shorter than its diff:
```python
import functools

import jax
import jax.numpy as jnp
from jax import lax
from jax.experimental import pallas as pl
from jax.experimental.pallas import tpu as pltpu
from jax.sharding import PartitionSpec as P

MESH = pl.DeviceIdType.MESH
F32, BF16 = jnp.float32, jnp.bfloat16
PARTS = 2
CHUNKS = 1


def far_first(n):
    return [n // 2 + (-(k + 1) // 2 if k % 2 else k // 2) for k in range(n)]


def dot(a, b, ca, cb):
    return lax.dot_general(a, b, (((ca,), (cb,)), ((), ())), preferred_element_type=F32)


def iota(shape, dim):
    return lax.broadcasted_iota(jnp.int32, shape, dim)


def kernel(
    side, reps, ids_hbm, gates_hbm, tok_hbm, up_hbm, down_hbm, out_ref,
    ids_v, gates_v, up_v, down_v, told, picked, inbound, part, gathered, hid,
    sent, back, mixed, shares, weight,
    s_load, s_tok, r_tok, s_pick, r_pick, s_part, r_part, s_hid, r_hid, s_out, r_out, s_mix, r_mix,
):
    top, toks = ids_v.shape
    experts = 2 * side * side
    width = tok_hbm.shape[1]
    ffc = up_v.shape[1] // CHUNKS
    lines = 2 * side
    held = side * toks
    e = lax.axis_index("ep")
    x = lax.axis_index("rep")
    y, z, c = e // lines, (e // 2) % side, e % 2
    p, q = y * (1 - c) + z * c, z * (1 - c) + y * c
    sp = lines * (1 - c) + 2 * c
    sq = 2 * (1 - c) + lines * c
    order = far_first(side)
    half = side // 2
    place = order[half:] + order[:half]
    blocks = [(s, other) for s in order for other in range(2)]
    per_group = lines // PARTS
    lot_rows = 2 * half
    rows = per_group * lot_rows
    per = rows // reps
    streams = range(2)
    parts = [range(PARTS)[::-1], range(PARTS)]
    groups = [(h, k) for h in streams for k in parts[h]]

    def off(v, s, n):
        return lax.rem(v + s % n, n)

    barrier = pltpu.get_barrier_semaphore()

    def greet(ep, rep):
        pl.semaphore_signal(barrier, inc=1, device_id=(ep, rep), device_id_type=MESH)

    for s in order[:-1]:
        for core in range(2):
            greet(y * lines + off(z, s, side) * 2 + core, x)
            greet(off(y, s, side) * lines + z * 2 + core, x)
    greet(e + 1 - 2 * c, x)
    rep_order = far_first(reps)[:-1]
    for s in rep_order:
        greet(e, off(x, s, reps))

    loads = [
        pltpu.make_async_copy(ids_hbm, ids_v, s_load.at[0]),
        pltpu.make_async_copy(gates_hbm, gates_v, s_load.at[1]),
        pltpu.make_async_copy(tok_hbm, told.at[half - 1, :, pl.ds(0, width)], s_load.at[2]),
        pltpu.make_async_copy(up_hbm.at[0], up_v, s_load.at[3]),
        pltpu.make_async_copy(down_hbm.at[0], down_v, s_load.at[4]),
    ]
    for load in loads:
        load.start()

    loads[0].wait()
    loads[1].wait()
    ids, gates = ids_v[...], gates_v[...]
    which = iota((experts, toks), 0)
    named = jnp.zeros((experts, toks), F32)
    gate = jnp.zeros((experts, toks), F32)
    for k in range(top):
        same = which == ids[k:k + 1, :]
        named = jnp.where(same, 1.0, named)
        gate = jnp.where(same, gates[k:k + 1, :], gate)
    earlier = (iota((toks, toks), 0) < iota((toks, toks), 1)).astype(BF16)
    rank = dot(named.astype(BF16), earlier, 1, 0)
    code = jnp.where(rank > 0.5, -gate, gate).astype(BF16)
    eye = (iota((experts, experts), 0) == iota((experts, experts), 1)).astype(BF16)
    told[half - 1, :, width:] = dot(code, eye, 0, 0).astype(BF16)
    loads[2].wait()
    pl.semaphore_wait(barrier, 4 * (side - 1) + 1 + reps - 1)

    started = []

    def send(src, dst, s_sem, r_sem, ep, rep):
        copy = pltpu.make_async_remote_copy(
            src_ref=src, dst_ref=dst, send_sem=s_sem, recv_sem=r_sem, device_id=(ep, rep), device_id_type=MESH)
        copy.start()
        started.append(copy)

    def arrival(ref, sem):
        pltpu.make_async_copy(ref, ref, sem).wait()

    own = half - 1
    for i, s in enumerate(place):
        if i == own:
            continue
        send(told.at[own], told.at[i], s_tok.at[i], r_tok.at[i], off(p, s, side) * sp + q * sq + c, x)

    def expert_of(row, first):
        block = first + row // lot_rows
        k = block // 2
        s = side // 2 + jnp.where(k % 2 == 1, -((k + 1) // 2), k // 2)
        return p * sp + lax.rem(q + s, side) * sq + jnp.where(block % 2 == 1, 1 - c, c)

    held = half * toks
    row, tok = iota((rows, held), 0), iota((rows, held), 1)
    mine = (row % lot_rows) // 2 == tok // toks
    sign = jnp.where(mine, (1 - 2 * (row % 2)).astype(F32), 0.0)
    for h in streams:
        mates = slice(h * half, (h + 1) * half)
        for i in range(h * half, (h + 1) * half):
            if i != own:
                arrival(told.at[i], r_tok.at[i])
        codes = told[mates, :, width:].reshape(held, experts)
        have = told[mates, :, :width].reshape(held, width)
        for k in parts[h]:
            sel = (expert_of(iota((rows, experts), 0), k * per_group) == iota((rows, experts), 1)).astype(BF16)
            pick = jnp.where(dot(sel, codes, 1, 1) * sign > 0.0, 1.0, 0.0).astype(BF16)
            lot = dot(pick, have, 1, 0).reshape(per_group, lot_rows, width).astype(BF16)
            picked[h, k * per_group:(k + 1) * per_group] = lot
            for j in range(k * per_group, (k + 1) * per_group):
                s, other = blocks[j]
                if (s, other) == (0, 0):
                    inbound[h, j] = lot[j - k * per_group]
                    continue
                core = 1 - c if other else c
                send(picked.at[h, j], inbound.at[h, j], s_pick.at[h, j], r_pick.at[h, j],
                     p * sp + off(q, s, side) * sq + core, x)

    every = lines * lot_rows
    col, tok = iota((held, every), 1), iota((held, every), 0)
    sel = (expert_of(iota((experts, every), 1), 0) == iota((experts, every), 0)).astype(BF16)
    for h in streams:
        codes = told[h * half:(h + 1) * half, :, width:].reshape(held, experts)
        value = dot(codes, sel, 1, 0) * (1 - 2 * (col % 2)).astype(F32)
        right = (value > 0.0) & ((col % lot_rows) // 2 == tok // toks)
        weight[h] = jnp.where(right, value, 0.0).astype(BF16)

    loads[3].wait()
    for g, (h, k) in enumerate(groups):
        for j in range(k * per_group, (k + 1) * per_group):
            if blocks[j] != (0, 0):
                arrival(inbound.at[h, j], r_pick.at[h, j])
        lhs = inbound[h, k * per_group:(k + 1) * per_group].astype(F32).reshape(rows, width).astype(BF16)
        for n in range(CHUNKS):
            cols = pl.ds(n * ffc, ffc)
            part[g, :, :, cols] = dot(lhs, up_v[:, cols], 1, 0).astype(BF16).reshape(reps, per, ffc)
            for s in rep_order:
                to = off(x, s, reps)
                send(part.at[g, to, :, cols], gathered.at[g, s, :, cols], s_part.at[g, s, n], r_part.at[g, s, n], e, to)

    for g in range(len(groups)):
        for n in range(CHUNKS):
            cols = pl.ds(n * ffc, ffc)
            for s in rep_order:
                arrival(gathered.at[g, s, :, cols], r_part.at[g, s, n])
            pre = part[g, x, :, cols].astype(F32)
            for s in range(1, reps):
                pre = pre + gathered[g, s, :, cols].astype(F32)
            hid[g, x, :, cols] = (pre / (1.0 + jnp.exp(-pre))).astype(BF16)
            for s in rep_order:
                send(hid.at[g, x, :, cols], hid.at[g, x, :, cols], s_hid.at[g, s, n], r_hid.at[g, s, n],
                     e, off(x, s, reps))

    loads[4].wait()
    for g, (h, k) in enumerate(groups):
        total = None
        for n in range(CHUNKS):
            cols = pl.ds(n * ffc, ffc)
            for s in rep_order:
                arrival(hid.at[g, off(x, -s, reps), :, cols], r_hid.at[g, s, n])
            term = dot(hid[g, :, :, cols].reshape(rows, ffc), down_v[cols, :], 1, 0)
            total = term if total is None else total + term
        lot = total.reshape(per_group, lot_rows, width).astype(BF16)
        sent[h, k * per_group:(k + 1) * per_group] = lot
        for j in range(k * per_group, (k + 1) * per_group):
            s, other = blocks[j]
            if (s, other) == (0, 0):
                back[h, j] = lot[j - k * per_group]
                continue
            if other:
                ep = off(p, -s, side) * sp + q * sq + 1 - c
            else:
                ep = p * sp + off(q, -s, side) * sq + c
            send(sent.at[h, j], back.at[h, j], s_out.at[h, j], r_out.at[h, j], ep, x)

    for h in streams:
        for j in range(lines):
            if blocks[j] != (0, 0):
                arrival(back.at[h, j], r_out.at[h, j])
        lot = dot(weight[h], back[h].astype(F32).reshape(every, width).astype(BF16), 1, 0)
        mixed[h * half:(h + 1) * half] = lot.astype(BF16).reshape(half, toks, width)
        for i in range(h * half, (h + 1) * half):
            if i != own:
                send(mixed.at[i], shares.at[i], s_mix.at[i], r_mix.at[i],
                     off(p, -place[i], side) * sp + q * sq + c, x)
    total = mixed[own].astype(F32)
    for i in range(side):
        if i != own:
            arrival(shares.at[i], r_mix.at[i])
            total = total + shares[i].astype(F32)
    out_ref[...] = total.astype(BF16)

    for copy in started:
        copy.wait_send()


def local(side, reps, tokens, expert_ids, gate_weights, up_weight, down_weight):
    toks, top = expert_ids.shape
    width = tokens.shape[1]
    ff = up_weight.shape[2]
    experts = 2 * side * side
    lines = 2 * side
    half = side // 2
    groups = 2 * PARTS
    per = lines * side // groups * 2 // reps
    anywhere = pl.BlockSpec(memory_space=pl.ANY)
    dma = pltpu.SemaphoreType.DMA
    vmem = pltpu.VMEM
    return pl.pallas_call(
        functools.partial(kernel, side, reps),
        out_shape=jax.ShapeDtypeStruct((toks, width), BF16),
        in_specs=[anywhere] * 5,
        out_specs=pl.BlockSpec(memory_space=pltpu.VMEM),
        scratch_shapes=[
            vmem((top, toks), jnp.int32),
            vmem((top, toks), F32),
            vmem((width, ff), BF16),
            vmem((ff, width), BF16),
            vmem((side, toks, width + experts), BF16),
            vmem((2, lines, side, width), BF16),
            vmem((2, lines, side, width), BF16),
            vmem((groups, reps, per, ff), BF16),
            vmem((groups, reps, per, ff), BF16),
            vmem((groups, reps, per, ff), BF16),
            vmem((2, lines, side, width), BF16),
            vmem((2, lines, side, width), BF16),
            vmem((side, toks, width), BF16),
            vmem((side, toks, width), BF16),
            vmem((2, half * toks, lines * side), BF16),
            dma((5,)),
            dma((side,)), dma((side,)),
            dma((2, lines)), dma((2, lines)),
            dma((groups, reps, CHUNKS)), dma((groups, reps, CHUNKS)),
            dma((groups, reps, CHUNKS)), dma((groups, reps, CHUNKS)),
            dma((2, lines)), dma((2, lines)),
            dma((side,)), dma((side,)),
        ],
        compiler_params=pltpu.CompilerParams(
            collective_id=0, has_side_effects=True, vmem_limit_bytes=40 * 1024 * 1024),
    )(*[pltpu.with_memory_space_constraint(v, pltpu.HBM) for v in (expert_ids.T, gate_weights.T, tokens, up_weight, down_weight)])


def solution(mesh):
    side = round((mesh.shape["ep"] // 2) ** 0.5)
    placed = (
        P("ep", "rep"),
        P("ep", None),
        P("ep", None),
        P("ep", "rep", None),
        P("ep", None, "rep"),
    )
    return jax.shard_map(
        functools.partial(local, side, mesh.shape["rep"]),
        mesh=mesh, in_specs=placed, out_specs=P("ep", "rep"), check_vma=False
    )
```

time: 143 us -> 52.4 us (0.37)
  waiting for transfers between devices: 63.3 us -> 0 us
  Pallas kernels: 0 us -> 51.6 us
  blocking collectives: 36.4 us -> 0 us
  starting transfers between devices: 16.5 us -> 0 us
  between operations: 13.5 us -> 0.01 us
  local copies, waits for them, and re-layouts: 6.8 us -> 0.61 us
  matrix products: 3.98 us -> 0 us
  other arithmetic: 1.97 us -> 0 us
    pallas_call x0 -> x1, Pallas kernels: none -> 51.6 us  [local(): pl.pallas_call(functools.partial(kernel, side, reps), out_shape=jax.Shape...]
    psum x1 -> x0, waiting for transfers between devices: 45.2 us -> none  [local(): lax.psum(partial_pre.astype(jnp.bfloat16), 'rep').astype(jnp.float32)]
    all_to_all x1 -> x0, blocking collectives: 36.4 us -> none  [local(): lax.all_to_all(outbound, 'ep', split_axis=0, concat_axis=0, tiled=True)]
    all_to_all x1 -> x0, waiting for transfers between devices: 18.1 us -> none  [local(): lax.all_to_all(expert_out, 'ep', split_axis=0, concat_axis=0, tiled=True)]
    all_to_all x1 -> x0, starting transfers between devices: 16.5 us -> none  [local(): lax.all_to_all(expert_out, 'ep', split_axis=0, concat_axis=0, tiled=True)]
    dot_general x2 -> x0, matrix products: 3.98 us -> none  [the longest x1 2.42 us: local(): jnp.dot(hidden, down_local, preferred_element_type=jnp.float32)]
    scatter x1 -> x0, local copies, waits for them, and re-layouts: 3.23 us -> none  [local(): outbound = jnp.zeros((n_peers * capacity, width_part), tokens.dtype).at[s...]
    all_to_all x4 -> x0, local copies, waits for them, and re-layouts: 1.46 us -> none  [the longest x2 1.12 us: local(): lax.all_to_all(expert_out, 'ep', split_axis=0, concat_axis=0, tiled=True)]
  transfers between devices with their start and end apart: 2 -> 0, of which waited for: 2 -> 0; matrix products, arithmetic and copies ran while one was open for 0% -> 0% of each run, Pallas kernels for 0% -> 0%
where the time goes in v2:
time: 52.4 us; the launch traced here: 52.2 us
  Pallas kernels  51.6 us (98%)
  local copies, waits for them, and re-layouts  0.61 us (1%)
    pallas_call x1, Pallas kernels, local(): pl.pallas_call(functools.partial(kernel, side, reps), out_shape=jax.Shape...  51.6 us

profile of v2, /device:TPU:1, one launch (start us, length us, event | category | flops | bytes accessed | tf_op | source)
XLA Modules:
  0.0 52.2 jit_solution(12560644332169543851)
XLA Ops:
  0.0 51.6 %shard_map.55 = bf16[16,896]{1,0:T(8,128)(2,1)S(1)} custom-call(s32[8,16]{1,0:T(8,128)} %bitcast.2, f32[8,16]{1,0:T(8,128)} %bitcast.3, bf16[16,896]{1,0:T(8,128)(2,1)} %tok_hbm.1, bf16[1,896,1024]{2,1,0:T(8,128)(2,1)} %up_hbm.1, bf16[1,1024,896]{2,1,0:T(8,128)(2,1)} %down_hbm.1), custom_call_target="tpu_custom_call" | custom-call | tf_op jit(solution)/shard_map/pallas_call | solution.py:241
  51.6 0.6 %copy.7 = bf16[16,896]{1,0:T(8,128)(2,1)} copy(bf16[16,896]{1,0:T(8,128)(2,1)S(1)} %shard_map.55) | data formatting | bytes 57344

commit v3 on v2

--- a/solution.py
+++ b/solution.py
@@ -9,7 +9,7 @@
 
 MESH = pl.DeviceIdType.MESH
 F32, BF16 = jnp.float32, jnp.bfloat16
-PARTS = 2
+PARTS = 4
 CHUNKS = 1
 
 
@@ -158,19 +158,21 @@
         weight[h] = jnp.where(right, value, 0.0).astype(BF16)
 
     loads[3].wait()
-    for g, (h, k) in enumerate(groups):
+
+    def up(g):
+        h, k = groups[g]
         for j in range(k * per_group, (k + 1) * per_group):
             if blocks[j] != (0, 0):
                 arrival(inbound.at[h, j], r_pick.at[h, j])
         lhs = inbound[h, k * per_group:(k + 1) * per_group].astype(F32).reshape(rows, width).astype(BF16)
         for n in range(CHUNKS):
             cols = pl.ds(n * ffc, ffc)
-            part[g, :, :, cols] = dot(lhs, up_v[:, cols], 1, 0).astype(BF16).reshape(reps, per, ffc)
+            part[g, :, :, cols] = dot(lhs, up_v[:, cols], 1, 0).reshape(reps, per, ffc).astype(BF16)
             for s in rep_order:
                 to = off(x, s, reps)
                 send(part.at[g, to, :, cols], gathered.at[g, s, :, cols], s_part.at[g, s, n], r_part.at[g, s, n], e, to)
 
-    for g in range(len(groups)):
+    def act(g):
         for n in range(CHUNKS):
             cols = pl.ds(n * ffc, ffc)
             for s in rep_order:
@@ -183,14 +185,14 @@
                 send(hid.at[g, x, :, cols], hid.at[g, x, :, cols], s_hid.at[g, s, n], r_hid.at[g, s, n],
                      e, off(x, s, reps))
 
-    loads[4].wait()
-    for g, (h, k) in enumerate(groups):
+    def down(g):
+        h, k = groups[g]
         total = None
         for n in range(CHUNKS):
             cols = pl.ds(n * ffc, ffc)
             for s in rep_order:
                 arrival(hid.at[g, off(x, -s, reps), :, cols], r_hid.at[g, s, n])
-            term = dot(hid[g, :, :, cols].reshape(rows, ffc), down_v[cols, :], 1, 0)
+            term = dot(hid[g, :, :, cols].astype(F32).reshape(rows, ffc).astype(BF16), down_v[cols, :], 1, 0)
             total = term if total is None else total + term
         lot = total.reshape(per_group, lot_rows, width).astype(BF16)
         sent[h, k * per_group:(k + 1) * per_group] = lot
@@ -205,6 +207,11 @@
                 ep = p * sp + off(q, -s, side) * sq + c
             send(sent.at[h, j], back.at[h, j], s_out.at[h, j], r_out.at[h, j], ep, x)
 
+    loads[4].wait()
+    for step in (up, act, down):
+        for g in range(len(groups)):
+            step(g)
+
     for h in streams:
         for j in range(lines):
             if blocks[j] != (0, 0):
@@ -215,6 +222,8 @@
             if i != own:
                 send(mixed.at[i], shares.at[i], s_mix.at[i], r_mix.at[i],
                      off(p, -place[i], side) * sp + q * sq + c, x)
+    for copy in started[:-(side - 1)]:
+        copy.wait_send()
     total = mixed[own].astype(F32)
     for i in range(side):
         if i != own:
@@ -222,7 +231,7 @@
             total = total + shares[i].astype(F32)
     out_ref[...] = total.astype(BF16)
 
-    for copy in started:
+    for copy in started[-(side - 1):]:
         copy.wait_send()
 
 

time: 52.4 us -> 52 us (level)
  no operation moved by 1% of the time
where the time goes in v3:
time: 52 us; the launch traced here: 51.8 us
  Pallas kernels  51.2 us (98%)
  local copies, waits for them, and re-layouts  0.61 us (1%)
    pallas_call x1, Pallas kernels, local(): pl.pallas_call(functools.partial(kernel, side, reps), out_shape=jax.Shape...  51.2 us

profile of v3, /device:TPU:1, one launch (start us, length us, event | category | flops | bytes accessed | tf_op | source)
XLA Modules:
  0.0 51.8 jit_solution(18112926941450529148)
XLA Ops:
  0.0 51.2 %shard_map.55 = bf16[16,896]{1,0:T(8,128)(2,1)S(1)} custom-call(s32[8,16]{1,0:T(8,128)} %bitcast.2, f32[8,16]{1,0:T(8,128)} %bitcast.3, bf16[16,896]{1,0:T(8,128)(2,1)} %tok_hbm.1, bf16[1,896,1024]{2,1,0:T(8,128)(2,1)} %up_hbm.1, bf16[1,1024,896]{2,1,0:T(8,128)(2,1)} %down_hbm.1), custom_call_target="tpu_custom_call" | custom-call | tf_op jit(solution)/shard_map/pallas_call | solution.py:250
  51.2 0.6 %copy.7 = bf16[16,896]{1,0:T(8,128)(2,1)} copy(bf16[16,896]{1,0:T(8,128)(2,1)S(1)} %shard_map.55) | data formatting | bytes 57344

commit v4 on v3

--- a/solution.py
+++ b/solution.py
@@ -58,6 +58,16 @@
     def off(v, s, n):
         return lax.rem(v + s % n, n)
 
+    loads = [
+        pltpu.make_async_copy(ids_hbm, ids_v, s_load.at[0]),
+        pltpu.make_async_copy(gates_hbm, gates_v, s_load.at[1]),
+        pltpu.make_async_copy(tok_hbm, told.at[half - 1, :, pl.ds(0, width)], s_load.at[2]),
+        pltpu.make_async_copy(up_hbm.at[0], up_v, s_load.at[3]),
+        pltpu.make_async_copy(down_hbm.at[0], down_v, s_load.at[4]),
+    ]
+    for load in loads[:3]:
+        load.start()
+
     barrier = pltpu.get_barrier_semaphore()
 
     def greet(ep, rep):
@@ -72,14 +82,7 @@
     for s in rep_order:
         greet(e, off(x, s, reps))
 
-    loads = [
-        pltpu.make_async_copy(ids_hbm, ids_v, s_load.at[0]),
-        pltpu.make_async_copy(gates_hbm, gates_v, s_load.at[1]),
-        pltpu.make_async_copy(tok_hbm, told.at[half - 1, :, pl.ds(0, width)], s_load.at[2]),
-        pltpu.make_async_copy(up_hbm.at[0], up_v, s_load.at[3]),
-        pltpu.make_async_copy(down_hbm.at[0], down_v, s_load.at[4]),
-    ]
-    for load in loads:
+    for load in loads[3:]:
         load.start()
 
     loads[0].wait()

time: 52 us -> 51.9 us (level)
  no operation moved by 1% of the time
where the time goes in v4:
time: 51.9 us; the launch traced here: 51.7 us
  Pallas kernels  51.1 us (98%)
  local copies, waits for them, and re-layouts  0.61 us (1%)
    pallas_call x1, Pallas kernels, local(): pl.pallas_call(functools.partial(kernel, side, reps), out_shape=jax.Shape...  51.1 us

profile of v4, /device:TPU:1, one launch (start us, length us, event | category | flops | bytes accessed | tf_op | source)
XLA Modules:
  0.0 51.7 jit_solution(3009227672901972565)
XLA Ops:
  0.0 51.1 %shard_map.55 = bf16[16,896]{1,0:T(8,128)(2,1)S(1)} custom-call(s32[8,16]{1,0:T(8,128)} %bitcast.2, f32[8,16]{1,0:T(8,128)} %bitcast.3, bf16[16,896]{1,0:T(8,128)(2,1)} %tok_hbm.1, bf16[1,896,1024]{2,1,0:T(8,128)(2,1)} %up_hbm.1, bf16[1,1024,896]{2,1,0:T(8,128)(2,1)} %down_hbm.1), custom_call_target="tpu_custom_call" | custom-call | tf_op jit(solution)/shard_map/pallas_call | solution.py:253
  51.1 0.6 %copy.7 = bf16[16,896]{1,0:T(8,128)(2,1)} copy(bf16[16,896]{1,0:T(8,128)(2,1)S(1)} %shard_map.55) | data formatting | bytes 57344
